TPU v7x, 128 devices: a whole 4x4x4 slice. The times are simulated.
128 devices in a mesh: row: 16 (over y, x), col: 4 (over z), dp: 2 (over core).
Axes of the slice: x: 4, y: 4, z: 4, core: 2. Of those that a mesh axis runs over, the one named last changes fastest.
Arguments:
- inputs: bfloat16 [1024, 8192], P(('col', 'dp'), 'row'), may hold values from -6 to 6
- gate_weight: bfloat16 [8192, 14336], P('row', 'col'), may hold values from -0.0625 to 0.0625
- up_weight: bfloat16 [8192, 14336], P('row', 'col'), may hold values from -0.0625 to 0.0625
- down_weight: bfloat16 [14336, 8192], P('col', 'row'), may hold values from -0.046875 to 0.046875
- reward_head: bfloat16 [8192], P('row'), may hold values from -0.0625 to 0.0625
- upstream: bfloat16 [1024, 8192], P(('col', 'dp'), 'row'), may hold values from -0.59765625 to 0.59765625
- labels: int32 [1024], P(('col', 'dp')), may hold values from 0 to 1
- label_mask: int32 [1024], P(('col', 'dp')), may hold values 0 or 1
Outputs:
- gate_grad: float32 [8192, 14336], P(('row', 'dp'), 'col')
- up_grad: float32 [8192, 14336], P(('row', 'dp'), 'col')
- down_grad: float32 [14336, 8192], P(('col', 'dp'), 'row')
- input_grad: float32 [1024, 8192], P(('col', 'dp'), 'row')
All inputs are finite; a program needn't handle non-finite values. No bound on the sum of `label_mask` on one device may be relied on, other than what follows from the above.
Results may differ from a plain program's by a relative error of at most 0.035.
Values may be sent and summed in bfloat16 or wider, within the bound.
No kernel may reach another device: no remote copies, remote signals or barrier semaphores. Data moves between devices by JAX's collectives and lax.ppermute only.
A program may use at most 128 MiB of HBM per device.

v0:
```python
import jax
import jax.numpy as jnp
from jax import lax
from jax.sharding import PartitionSpec as P

reward_weight = 8.0
BF = jnp.bfloat16
F32 = jnp.float32


def transpose_product(left, right):
    return lax.dot_general(left, right, (((0,), (0,)), ((), ())), preferred_element_type=F32)


def right_transpose(left, right):
    return lax.dot_general(left, right, (((1,), (1,)), ((), ())), preferred_element_type=F32)


def per_device(
    inputs, gate_weight, up_weight, down_weight, reward_head, upstream, labels, label_mask
):
    tokens, depth = inputs.shape
    half = gate_weight.shape[1] // 2
    n_row = lax.axis_size("row")
    core = lax.axis_index("dp")
    row = lax.axis_index("row")
    token_axes = ("col", "dp")
    tags = jnp.stack([labels, label_mask], axis=1).astype(BF)
    tags = jnp.pad(tags, ((0, 0), (0, 126)))
    packed = jnp.concatenate([inputs, upstream, tags], axis=1)
    everyone = lax.all_gather(packed, token_axes, axis=0, tiled=True)
    x_all = everyone[:, :depth]
    upstream_all = everyone[:, depth : 2 * depth]
    total = x_all.shape[0]
    mine = total // n_row
    gate_half = lax.dynamic_slice_in_dim(gate_weight, core * half, half, 1)
    up_half = lax.dynamic_slice_in_dim(up_weight, core * half, half, 1)
    down_half = lax.dynamic_slice_in_dim(down_weight, core * half, half, 0)
    head_value = reward_head.astype(F32)
    head_hidden = jnp.dot(down_half.astype(F32), head_value, precision=lax.Precision.HIGHEST)
    head_inputs = jnp.dot(x_all.astype(F32), head_value, precision=lax.Precision.HIGHEST)
    per_token = half // mine
    extras = jnp.concatenate(
        [
            head_inputs[:, None],
            jnp.tile(head_hidden.reshape(mine, per_token), (n_row, 1)),
            jnp.zeros((total, 127 - per_token), F32),
        ],
        axis=1,
    )
    partial = jnp.concatenate(
        [
            jnp.dot(x_all, gate_half, preferred_element_type=F32).astype(BF),
            jnp.dot(x_all, up_half, preferred_element_type=F32).astype(BF),
            right_transpose(upstream_all, down_half).astype(BF),
            extras.astype(BF),
        ],
        axis=1,
    )
    summed = lax.psum_scatter(partial, "row", scatter_dimension=0, tiled=True).astype(F32)
    gate = summed[:, :half]
    upper = summed[:, half : 2 * half]
    grad_upstream = summed[:, 2 * half : 3 * half]
    extra = summed[:, 3 * half :]
    head_hidden = extra[:, 1 : 1 + per_token].reshape(half)
    sigmoid_gate = jax.nn.sigmoid(gate)
    hidden = (gate * sigmoid_gate * upper).astype(BF)
    score = extra[:, 0] + lax.psum(
        jnp.sum(hidden.astype(F32) * head_hidden[None, :], axis=1), token_axes
    )
    own_tags = lax.dynamic_slice_in_dim(everyone[:, 2 * depth :], row * mine, mine, 0).astype(F32)
    slope = reward_weight * own_tags[:, 1] * (jax.nn.sigmoid(score) - own_tags[:, 0])
    grad_hidden = grad_upstream + slope[:, None] * head_hidden[None, :]
    grad_gate = (grad_hidden * upper * sigmoid_gate * (1.0 + gate * (1.0 - sigmoid_gate))).astype(
        BF
    )
    grad_upper = (grad_hidden * gate * sigmoid_gate).astype(BF)
    slope_high = slope.astype(BF)
    slope_low = (slope - slope_high.astype(F32)).astype(BF)
    slopes = jnp.pad(jnp.stack([slope_high, slope_low], axis=1), ((0, 0), (0, 126)))
    gathered = lax.all_gather(
        jnp.concatenate([hidden, grad_gate, grad_upper, slopes], axis=1), "row", axis=0, tiled=True
    )
    hidden_all = gathered[:, :half]
    grad_gate_all = gathered[:, half : 2 * half]
    grad_upper_all = gathered[:, 2 * half : 3 * half]
    slope_all = gathered[:, 3 * half].astype(F32) + gathered[:, 3 * half + 1].astype(F32)
    input_part = right_transpose(grad_gate_all, gate_half) + right_transpose(
        grad_upper_all, up_half
    )
    input_sum = lax.psum_scatter(
        input_part.astype(BF), token_axes, scatter_dimension=0, tiled=True
    ).astype(F32)
    place = (lax.axis_index("col") * 2 + core) * tokens
    own_slope = lax.dynamic_slice_in_dim(slope_all, place, tokens, 0)
    input_grad = upstream.astype(F32) + own_slope[:, None] * head_value[None, :] + input_sum
    grad_mixed = (upstream_all.astype(F32) + slope_all[:, None] * head_value[None, :]).astype(BF)
    down_grad = transpose_product(hidden_all, grad_mixed)

    def both_halves(part):
        keep = lax.dynamic_slice_in_dim(part, core * (depth // 2), depth // 2, 0)
        send = lax.dynamic_slice_in_dim(part, (1 - core) * (depth // 2), depth // 2, 0)
        other = lax.ppermute(send.astype(BF), "dp", [(0, 1), (1, 0)]).astype(F32)
        first = core == 0
        return jnp.concatenate(
            [jnp.where(first, keep, other), jnp.where(first, other, keep)], axis=1
        )

    gate_grad = both_halves(transpose_product(x_all, grad_gate_all))
    up_grad = both_halves(transpose_product(x_all, grad_upper_all))
    return (gate_grad, up_grad, down_grad, input_grad)


def solution(mesh):
    in_specs = (
        P(("col", "dp"), "row"),
        P("row", "col"),
        P("row", "col"),
        P("col", "row"),
        P("row"),
        P(("col", "dp"), "row"),
        P(("col", "dp")),
        P(("col", "dp")),
    )
    out_specs = (
        P(("row", "dp"), "col"),
        P(("row", "dp"), "col"),
        P(("col", "dp"), "row"),
        P(("col", "dp"), "row"),
    )
    return jax.shard_map(
        per_device, mesh=mesh, in_specs=in_specs, out_specs=out_specs, check_vma=False
    )
```

profile of v0, /device:TPU:0, one launch (start us, length us, event | category | flops | bytes accessed | tf_op | source)
XLA Modules:
  0.0 312.7 jit_solution(9628465307973189131)
XLA Ops:
  8.0 1.7 fusion.37
  10.5 2.1 fusion.22
  12.7 25.9 %all-gather.3.cloned.1.call-done = bf16[1024,1152]{1,0:T(8,128)(2,1)} async-done(((bf16[128,1152]{1,0:T(8,128)(2,1)}), bf16[1024,1152]{1,0:T(8,128)(2,1)}) %all-gather.3.cloned.1.call-update) | async-done | bytes 2359312 | tf_op jit(solution)/shard_map/all_gather | solution.py:31
  38.6 1.6 fusion.33
  40.4 5.9 %convolution_convert_fusion = bf16[1024,1792]{1,0:T(8,128)(2,1)} fusion(bf16[3584,512]{1,0:T(8,128)(2,1)} %param.11, s32[]{:T(128)S(6)} %select_n.40, bf16[1024,1152]{1,0:T(8,128)(2,1)} %all-gather.3.cloned.1.call-done), kind=kOutput, calls=%fused_computation | convolution fusion | flops 1880883200 | bytes 6553604 | tf_op jit(solution)/shard_map/dot_general | solution.py:16
  46.4 3.9 %convolution_convert_fusion.1 = bf16[1024,1792]{1,0:T(8,128)(2,1)} fusion(bf16[512,3584]{1,0:T(8,128)(2,1)S(1)} %copy-done.4, s32[]{:T(128)S(6)} %select_n.40, bf16[1024,1152]{1,0:T(8,128)(2,1)S(1)} %copy-done), kind=kOutput, calls=%fused_computation.1 | convolution fusion | flops 1880883200 | bytes 6553604 | tf_op jit(solution)/shard_map/dot_general | solution.py:54
  50.3 3.9 %convolution_convert_fusion.2 = bf16[1024,1792]{1,0:T(8,128)(2,1)} fusion(bf16[512,3584]{1,0:T(8,128)(2,1)S(1)} %copy-done.5, s32[]{:T(128)S(6)} %select_n.40, bf16[1024,1152]{1,0:T(8,128)(2,1)S(1)} %copy-done), kind=kOutput, calls=%fused_computation.2 | convolution fusion | flops 1880883200 | bytes 6553604 | tf_op jit(solution)/shard_map/dot_general | solution.py:53
  54.3 18.4 %concatenate.19 = bf16[1024,5504]{1,0:T(8,128)(2,1)} concatenate(bf16[1024,1792]{1,0:T(8,128)(2,1)} %convolution_convert_fusion.2, bf16[1024,1792]{1,0:T(8,128)(2,1)} %convolution_convert_fusion.1, bf16[1024,1792]{1,0:T(8,128)(2,1)} %convolution_convert_fusion, bf16[1024,1]{1,0:T(8,128)(2,1)S(1)} %broadcast_in_dim.14, bf16[1024,28]{1,0:T(8,128)(2,1)S(1)} %bitcast.12, ...), dimensions={1} | concatenate | bytes 22544384 | tf_op jit(solution)/shard_map/concatenate | solution.py:51
  72.7 0.9 slice-done
  73.8 90.5 %reduce-scatter.3.cloned.1.call-done = bf16[64,5504]{1,0:T(8,128)(2,1)} async-done(((bf16[1024,5504]{1,0:T(8,128)(2,1)}), bf16[64,5504]{1,0:T(8,128)(2,1)}) %reduce-scatter.3.cloned.1.call-update) | async-done | bytes 704528 | tf_op jit(solution)/shard_map/reduce_scatter | solution.py:60
  165.2 1.2 convert_element_type.87
  166.8 14.2 %psum.7 = f32[64]{0:T(128)S(1)} all-reduce(f32[64]{0:T(128)S(1)} %get-tuple-element.8), channel_id=1, replica_groups=mesh['row'=16,'col'=4,'dp'=2] {'col','dp'}, use_global_device_ids=true, to_apply=%region_2.3 | all-reduce | flops 64 | bytes 512 | tf_op jit(solution)/shard_map/psum | solution.py:68
  181.4 0.9 fusion.29
  182.4 80.0 %all-gather.5.cloned.1.call-done = bf16[1024,5504]{1,0:T(8,128)(2,1)} async-done(((bf16[64,5504]{1,0:T(8,128)(2,1)}), bf16[1024,5504]{1,0:T(8,128)(2,1)}) %all-gather.5.cloned.1.call-update) | async-done | bytes 11272208 | tf_op jit(solution)/shard_map/all_gather | solution.py:81
  262.4 4.8 %fusion.2 = f32[1024,512]{1,0:T(8,128)S(1)} fusion(bf16[1024,5504]{1,0:T(8,128)(2,1)} %all-gather.5.cloned.1.call-done, bf16[512,3584]{1,0:T(8,128)(2,1)} %param.10, s32[]{:T(128)S(6)} %select_n.40), kind=kOutput, calls=%fused_computation.7 | convolution fusion | flops 1879048192 | bytes 7602180 | tf_op jit(solution)/shard_map/dot_general | solution.py:16
  267.3 5.2 %add_convert_fusion = bf16[1024,512]{1,0:T(8,128)(2,1)} fusion(f32[1024,512]{1,0:T(8,128)S(1)} %fusion.2, bf16[512,3584]{1,0:T(8,128)(2,1)S(1)} %copy-done.6, s32[]{:T(128)S(6)} %select_n.40, bf16[1024,5504]{1,0:T(8,128)(2,1)} %all-gather.5.cloned.1.call-done), kind=kOutput, calls=%fused_computation.19 | convolution fusion | flops 1880096768 | bytes 8650756 | tf_op jit(solution)/shard_map/dot_general | solution.py:16
  272.5 4.2 %fusion.4 = f32[512,1792]{1,0:T(8,128)S(1)} fusion(bf16[1024,5504]{1,0:T(8,128)(2,1)} %all-gather.5.cloned.1.call-done, bf16[1024,1152]{1,0:T(8,128)(2,1)S(1)} %copy-done.1), kind=kOutput, calls=%fused_computation.9 | convolution fusion | flops 1879048192 | bytes 8388608 | tf_op jit(solution)/shard_map/dot_general | solution.py:12
  277.1 4.1 %fusion.8 = f32[512,1792]{1,0:T(8,128)S(1)} fusion(bf16[1024,5504]{1,0:T(8,128)(2,1)} %all-gather.5.cloned.1.call-done, bf16[1024,1152]{1,0:T(8,128)(2,1)S(1)} %copy-done.1), kind=kOutput, calls=%fused_computation.13 | convolution fusion | flops 1879048192 | bytes 8388608 | tf_op jit(solution)/shard_map/dot_general | solution.py:12
  281.9 1.5 convert_add_fusion
  283.6 6.1 %fusion = f32[1792,512]{1,0:T(8,128)} fusion(bf16[1024,5504]{1,0:T(8,128)(2,1)} %all-gather.5.cloned.1.call-done, f32[512]{0:T(512)S(1)} %convert_element_type.103, f32[1024]{0:T(1024)S(1)} %get-tuple-element.11, bf16[1024,1152]{1,0:T(8,128)(2,1)S(1)} %copy-done.1), kind=kOutput, calls=%fused_computation.3 | convolution fusion | flops 1881145344 | bytes 8394752 | tf_op jit(solution)/shard_map/dot_general | solution.py:12
  289.9 2.3 pad_maximum_fusion.1
  292.5 2.3 pad_maximum_fusion
  294.8 9.6 %reduce-scatter.5.cloned.1.call-done = bf16[128,512]{1,0:T(8,128)(2,1)} async-done(((bf16[1024,512]{1,0:T(8,128)(2,1)}), bf16[128,512]{1,0:T(8,128)(2,1)}) %reduce-scatter.5.cloned.1.call-update) | async-done | bytes 131088 | tf_op jit(solution)/shard_map/reduce_scatter | solution.py:91
  304.4 1.7 convert_add_fusion.1
  (53 shorter events, 5.7 us)
Async XLA Ops:
  7.2 31.4 %all-gather.3.cloned.1.call-start = ((), (), s32[]{:S(2)}) async-start(), calls=%async_computation.2 | async-start | bytes 2654208 | tf_op jit(solution)/shard_map/all_gather | solution.py:31
  9.8 154.5 %reduce-scatter.3.cloned.1.call-start = ((), (), s32[]{:S(2)}) async-start(), calls=%async_computation.3 | async-start | bytes 11976704 | tf_op jit(solution)/shard_map/reduce_scatter | solution.py:60
  40.4 5.9 %copy-start = (bf16[1024,1152]{1,0:T(8,128)(2,1)S(1)}, bf16[1024,1152]{1,0:T(8,128)(2,1)}, u32[]{:S(2)}) copy-start(bf16[1024,1152]{1,0:T(8,128)(2,1)} %all-gather.3.cloned.1.call-done) | copy-start | bytes 7077892
  40.4 5.9 %copy-start.4 = (bf16[512,3584]{1,0:T(8,128)(2,1)S(1)}, bf16[512,3584]{1,0:T(8,128)(2,1)}, u32[]{:S(2)}) copy-start(bf16[512,3584]{1,0:T(8,128)(2,1)} %param.10) | copy-start | bytes 11010052
  46.4 3.9 %copy-start.5 = (bf16[512,3584]{1,0:T(8,128)(2,1)S(1)}, bf16[512,3584]{1,0:T(8,128)(2,1)}, u32[]{:S(2)}) copy-start(bf16[512,3584]{1,0:T(8,128)(2,1)} %param.9) | copy-start | bytes 11010052
  72.6 0.9 slice-start
  72.7 189.7 %all-gather.5.cloned.1.call-start = ((), (), s32[]{:S(2)}) async-start(), calls=%async_computation.4 | async-start | bytes 11976704 | tf_op jit(solution)/shard_map/all_gather | solution.py:81
  166.5 15.9 %copy-start.3 = (bf16[512]{0:T(512)(128)(2,1)S(1)}, bf16[512]{0:T(512)(128)(2,1)}, u32[]{:S(2)}) copy-start(bf16[512]{0:T(512)(128)(2,1)} %param.12) | copy-start | bytes 3076
  182.3 122.1 %reduce-scatter.5.cloned.1.call-start = ((), (), s32[]{:S(2)}) async-start(), calls=%async_computation.5 | async-start | bytes 1179648 | tf_op jit(solution)/shard_map/reduce_scatter | solution.py:91
  262.4 4.9 %copy-start.6 = (bf16[512,3584]{1,0:T(8,128)(2,1)S(1)}, bf16[512,3584]{1,0:T(8,128)(2,1)}, u32[]{:S(2)}) copy-start(bf16[512,3584]{1,0:T(8,128)(2,1)} %param.9) | copy-start | bytes 11010052
  267.2 5.3 %copy-start.1 = (bf16[1024,1152]{1,0:T(8,128)(2,1)S(1)}, bf16[1024,1152]{1,0:T(8,128)(2,1)}, u32[]{:S(2)}) copy-start(bf16[1024,1152]{1,0:T(8,128)(2,1)} %all-gather.3.cloned.1.call-done) | copy-start | bytes 7077892
  276.8 12.8 %collective-permute-start.1 = (bf16[256,1792]{1,0:T(8,128)(2,1)S(1)}, bf16[256,1792]{1,0:T(8,128)(2,1)S(1)}, u32[]{:S(2)}, u32[]{:S(2)}) collective-permute-start(bf16[256,1792]{1,0:T(8,128)(2,1)S(1)} %dynamic-slice_convert_fusion), channel_id=1, source_target_pairs={{0,1},{1,0},{2,3},{3,2},{4,5},{5,4},{6,7},{7,6},{8,9},{9,8},{10,11... | collective-permute-start | bytes 2752520 | tf_op jit(solution)/shard_map/ppermute | solution.py:103
  281.3 10.9 %collective-permute-start = (bf16[256,1792]{1,0:T(8,128)(2,1)S(1)}, bf16[256,1792]{1,0:T(8,128)(2,1)S(1)}, u32[]{:S(2)}, u32[]{:S(2)}) collective-permute-start(bf16[256,1792]{1,0:T(8,128)(2,1)S(1)} %dynamic-slice_convert_fusion.1), channel_id=1, source_target_pairs={{0,1},{1,0},{2,3},{3,2},{4,5},{5,4},{6,7},{7,6},{8,9},{9,8},{10,11... | collective-permute-start | bytes 2752520 | tf_op jit(solution)/shard_map/ppermute | solution.py:103
  292.5 12.0 %copy-start.2 = (bf16[128,512]{1,0:T(8,128)(2,1)S(1)}, bf16[128,512]{1,0:T(8,128)(2,1)}, u32[]{:S(2)}) copy-start(bf16[128,512]{1,0:T(8,128)(2,1)} %param.13) | copy-start | bytes 393220
Sparse Core Ops, SparseCore 0:
  10.3 28.2 all-gather.2
  72.8 91.4 reduce-scatter.2
  182.4 79.9 all-gather.4
  272.6 31.7 reduce-scatter.4
where the time goes:
time: 314 us; the launch traced here: 313 us
  waiting for transfers between devices  206 us (66%)
  matrix products  41.9 us (13%)
  local copies, waits for them, and re-layouts  21.9 us (7%)
  blocking collectives  14.2 us (5%)
  between operations  14 us (4%)
  other arithmetic  13.6 us (4%)
    reduce_scatter x1, waiting for transfers between devices, per_device(): lax.psum_scatter(partial, 'row', scatter_dimension=0, tiled=True)  90.5 us
    all_gather x1, waiting for transfers between devices, per_device(): lax.all_gather(jnp.concatenate([hidden, grad_gate, grad_upper, slopes], a...  80 us
    all_gather x1, waiting for transfers between devices, per_device(): everyone = lax.all_gather(packed, token_axes, axis=0, tiled=True)  25.9 us
    concatenate x1, local copies, waits for them, and re-layouts, per_device(): jnp.concatenate([jnp.dot(x_all, gate_half, preferred_element_type=F32).as...  18.4 us
    dot_general x3, matrix products, right_transpose(): lax.dot_general(left, right, (((1,), (1,)), ((), ())), preferred_element_...  16 us
    dot_general x3, matrix products, transpose_product(): lax.dot_general(left, right, (((0,), (0,)), ((), ())), preferred_element_...  14.4 us
    psum x1, blocking collectives, per_device(): lax.psum(jnp.sum(hidden.astype(F32) * head_hidden[None, :], axis=1), toke...  14.2 us
    reduce_scatter x1, waiting for transfers between devices, per_device(): lax.psum_scatter(input_part.astype(BF), token_axes, scatter_dimension=0,...  9.63 us
  transfers between devices with their start and end apart: 6, of which 4 were waited for; matrix products, arithmetic and copies ran while one was open for 8% of the time, Pallas kernels for 0%

commit v1 on v0

--- a/solution.py
+++ b/solution.py
@@ -28,7 +28,15 @@
     tags = jnp.stack([labels, label_mask], axis=1).astype(BF)
     tags = jnp.pad(tags, ((0, 0), (0, 126)))
     packed = jnp.concatenate([inputs, upstream, tags], axis=1)
-    everyone = lax.all_gather(packed, token_axes, axis=0, tiled=True)
+    everyone = jnp.concatenate(
+        lax.all_to_all(
+            jnp.stack(lax.psum(1, axis_name=token_axes) * [packed]),
+            split_axis=0,
+            concat_axis=0,
+            axis_name=token_axes,
+        ),
+        axis=0,
+    )
     x_all = everyone[:, :depth]
     upstream_all = everyone[:, depth : 2 * depth]
     total = x_all.shape[0]

time: 314 us -> 323 us (1.029)
  starting transfers between devices: 1 us -> 6.49 us
    all_to_all x0 -> x1, waiting for transfers between devices: none -> 27.7 us  [per_device(): lax.all_to_all(jnp.stack(lax.psum(1, axis_name=token_axes) * [packed]), s...]
    all_gather x1 -> x0, waiting for transfers between devices: 25.9 us -> none  [per_device(): everyone = lax.all_gather(packed, token_axes, axis=0, tiled=True)]
    all_to_all x0 -> x1, starting transfers between devices: none -> 5.53 us  [per_device(): lax.all_to_all(jnp.stack(lax.psum(1, axis_name=token_axes) * [packed]), s...]
  transfers between devices with their start and end apart: 6 -> 6, of which waited for: 4 -> 4; matrix products, arithmetic and copies ran while one was open for 8% -> 7% of each run, Pallas kernels for 0% -> 0%
where the time goes in v1:
time: 323 us; the launch traced here: 322 us
  waiting for transfers between devices  208 us (64%)
  matrix products  41.9 us (13%)
  local copies, waits for them, and re-layouts  24.9 us (8%)
  blocking collectives  14.2 us (4%)
  between operations  14 us (4%)
  other arithmetic  12.8 us (4%)
  starting transfers between devices  6.49 us (2%)
    reduce_scatter x1, waiting for transfers between devices, per_device(): lax.psum_scatter(partial, 'row', scatter_dimension=0, tiled=True)  90.5 us
    all_gather x1, waiting for transfers between devices, per_device(): lax.all_gather(jnp.concatenate([hidden, grad_gate, grad_upper, slopes], a...  80 us
    all_to_all x1, waiting for transfers between devices, per_device(): lax.all_to_all(jnp.stack(lax.psum(1, axis_name=token_axes) * [packed]), s...  27.7 us
    concatenate x1, local copies, waits for them, and re-layouts, per_device(): jnp.concatenate([jnp.dot(x_all, gate_half, preferred_element_type=F32).as...  18.3 us
    dot_general x3, matrix products, right_transpose(): lax.dot_general(left, right, (((1,), (1,)), ((), ())), preferred_element_...  16 us
    dot_general x3, matrix products, transpose_product(): lax.dot_general(left, right, (((0,), (0,)), ((), ())), preferred_element_...  14.4 us
    psum x1, blocking collectives, per_device(): lax.psum(jnp.sum(hidden.astype(F32) * head_hidden[None, :], axis=1), toke...  14.2 us
    reduce_scatter x1, waiting for transfers between devices, per_device(): lax.psum_scatter(input_part.astype(BF), token_axes, scatter_dimension=0,...  9.73 us
  transfers between devices with their start and end apart: 6, of which 4 were waited for; matrix products, arithmetic and copies ran while one was open for 7% of the time, Pallas kernels for 0%

profile of v1, /device:TPU:0, one launch (start us, length us, event | category | flops | bytes accessed | tf_op | source)
XLA Modules:
  0.0 322.3 jit_solution(14505190267821144953)
XLA Ops:
  9.2 1.7 stack.35
  10.9 5.5 %all-to-all-start = ((bf16[8,128,1152]{1,2,0:T(8,128)(2,1)}), bf16[8,128,1152]{1,2,0:T(8,128)(2,1)S(1)}, u32[]{:S(2)}, u32[]{:S(2)}) async-start(bf16[8,128,1152]{1,2,0:T(8,128)(2,1)} %stack.35), calls=%async_computation | async-start | bytes 4718592 | tf_op jit(solution)/shard_map/all_to_all | solution.py:32
  16.5 2.1 fusion.22
  18.7 27.7 %all-to-all-done = bf16[8,128,1152]{1,2,0:T(8,128)(2,1)S(1)} async-done(((bf16[8,128,1152]{1,2,0:T(8,128)(2,1)}), bf16[8,128,1152]{1,2,0:T(8,128)(2,1)S(1)}, u32[]{:S(2)}, u32[]{:S(2)}) %all-to-all-start) | async-done | bytes 2359328 | tf_op jit(solution)/shard_map/all_to_all | solution.py:32
  46.5 2.6 copy.32
  49.0 1.6 fusion.33
  50.6 5.9 %convolution_convert_fusion = bf16[1024,1792]{1,0:T(8,128)(2,1)} fusion(bf16[3584,512]{1,0:T(8,128)(2,1)} %param.11, s32[]{:T(128)S(6)} %select_n.40, bf16[1024,1152]{1,0:T(8,128)(2,1)} %bitcast.14), kind=kOutput, calls=%fused_computation | convolution fusion | flops 1880883200 | bytes 6553604 | tf_op jit(solution)/shard_map/dot_general | solution.py:16
  56.8 3.9 %convolution_convert_fusion.1 = bf16[1024,1792]{1,0:T(8,128)(2,1)} fusion(bf16[512,3584]{1,0:T(8,128)(2,1)S(1)} %copy-done.4, s32[]{:T(128)S(6)} %select_n.40, bf16[1024,1152]{1,0:T(8,128)(2,1)S(1)} %bitcast.15), kind=kOutput, calls=%fused_computation.1 | convolution fusion | flops 1880883200 | bytes 6553604 | tf_op jit(solution)/shard_map/dot_general | solution.py:62
  60.7 3.9 %convolution_convert_fusion.2 = bf16[1024,1792]{1,0:T(8,128)(2,1)} fusion(bf16[512,3584]{1,0:T(8,128)(2,1)S(1)} %copy-done.5, s32[]{:T(128)S(6)} %select_n.40, bf16[1024,1152]{1,0:T(8,128)(2,1)S(1)} %bitcast.16), kind=kOutput, calls=%fused_computation.2 | convolution fusion | flops 1880883200 | bytes 6553604 | tf_op jit(solution)/shard_map/dot_general | solution.py:61
  64.7 18.3 %concatenate.19 = bf16[1024,5504]{1,0:T(8,128)(2,1)} concatenate(bf16[1024,1792]{1,0:T(8,128)(2,1)} %convolution_convert_fusion.2, bf16[1024,1792]{1,0:T(8,128)(2,1)} %convolution_convert_fusion.1, bf16[1024,1792]{1,0:T(8,128)(2,1)} %convolution_convert_fusion, bf16[1024,1]{1,0:T(8,128)(2,1)S(1)} %broadcast_in_dim.14, bf16[1024,28]{1,0:T(8,128)(2,1)S(1)} %bitcast.21, ...), dimensions={1} | concatenate | bytes 22544384 | tf_op jit(solution)/shard_map/concatenate | solution.py:59
  83.4 90.5 %reduce-scatter.3.cloned.1.call-done = bf16[64,5504]{1,0:T(8,128)(2,1)} async-done(((bf16[1024,5504]{1,0:T(8,128)(2,1)}), bf16[64,5504]{1,0:T(8,128)(2,1)}) %reduce-scatter.3.cloned.1.call-update) | async-done | bytes 704528 | tf_op jit(solution)/shard_map/reduce_scatter | solution.py:68
  174.8 1.2 convert_element_type.87
  176.3 14.2 %psum.7 = f32[64]{0:T(128)S(1)} all-reduce(f32[64]{0:T(128)S(1)} %get-tuple-element.8), channel_id=1, replica_groups=mesh['row'=16,'col'=4,'dp'=2] {'col','dp'}, use_global_device_ids=true, to_apply=%region_2.3 | all-reduce | flops 64 | bytes 512 | tf_op jit(solution)/shard_map/psum | solution.py:76
  192.0 80.0 %all-gather.2.cloned.1.call-done = bf16[1024,5504]{1,0:T(8,128)(2,1)} async-done(((bf16[64,5504]{1,0:T(8,128)(2,1)}), bf16[1024,5504]{1,0:T(8,128)(2,1)}) %all-gather.2.cloned.1.call-update) | async-done | bytes 11272208 | tf_op jit(solution)/shard_map/all_gather | solution.py:89
  272.0 4.8 %fusion.2 = f32[1024,512]{1,0:T(8,128)S(1)} fusion(bf16[1024,5504]{1,0:T(8,128)(2,1)} %all-gather.2.cloned.1.call-done, bf16[512,3584]{1,0:T(8,128)(2,1)} %param.10, s32[]{:T(128)S(6)} %select_n.40), kind=kOutput, calls=%fused_computation.7 | convolution fusion | flops 1879048192 | bytes 7602180 | tf_op jit(solution)/shard_map/dot_general | solution.py:16
  276.9 5.3 %add_convert_fusion = bf16[1024,512]{1,0:T(8,128)(2,1)} fusion(f32[1024,512]{1,0:T(8,128)S(1)} %fusion.2, bf16[512,3584]{1,0:T(8,128)(2,1)S(1)} %copy-done.6, s32[]{:T(128)S(6)} %select_n.40, bf16[1024,5504]{1,0:T(8,128)(2,1)} %all-gather.2.cloned.1.call-done), kind=kOutput, calls=%fused_computation.19 | convolution fusion | flops 1880096768 | bytes 8650756 | tf_op jit(solution)/shard_map/dot_general | solution.py:16
  282.2 4.2 %fusion.4 = f32[512,1792]{1,0:T(8,128)S(1)} fusion(bf16[1024,5504]{1,0:T(8,128)(2,1)} %all-gather.2.cloned.1.call-done, bf16[1024,1152]{1,0:T(8,128)(2,1)S(1)} %bitcast.18), kind=kOutput, calls=%fused_computation.9 | convolution fusion | flops 1879048192 | bytes 8388608 | tf_op jit(solution)/shard_map/dot_general | solution.py:12
  286.7 4.1 %fusion.8 = f32[512,1792]{1,0:T(8,128)S(1)} fusion(bf16[1024,5504]{1,0:T(8,128)(2,1)} %all-gather.2.cloned.1.call-done, bf16[1024,1152]{1,0:T(8,128)(2,1)S(1)} %bitcast.19), kind=kOutput, calls=%fused_computation.13 | convolution fusion | flops 1879048192 | bytes 8388608 | tf_op jit(solution)/shard_map/dot_general | solution.py:12
  291.5 1.4 convert_add_fusion
  293.1 6.1 %fusion = f32[1792,512]{1,0:T(8,128)} fusion(bf16[1024,5504]{1,0:T(8,128)(2,1)} %all-gather.2.cloned.1.call-done, f32[512]{0:T(512)S(1)} %convert_element_type.103, f32[1024]{0:T(1024)S(1)} %get-tuple-element.11, bf16[1024,1152]{1,0:T(8,128)(2,1)S(1)} %bitcast.20), kind=kOutput, calls=%fused_computation.3 | convolution fusion | flops 1881145344 | bytes 8394752 | tf_op jit(solution)/shard_map/dot_general | solution.py:12
  299.4 2.3 pad_maximum_fusion.1
  302.0 2.3 pad_maximum_fusion
  304.3 9.7 %reduce-scatter.5.cloned.1.call-done = bf16[128,512]{1,0:T(8,128)(2,1)} async-done(((bf16[1024,512]{1,0:T(8,128)(2,1)}), bf16[128,512]{1,0:T(8,128)(2,1)}) %reduce-scatter.5.cloned.1.call-update) | async-done | bytes 131088 | tf_op jit(solution)/shard_map/reduce_scatter | solution.py:99
  314.0 1.7 convert_add_fusion.1
  (54 shorter events, 7.1 us)
Async XLA Ops:
  10.9 5.6 %copy-start.3 = (bf16[512]{0:T(512)(128)(2,1)S(1)}, bf16[512]{0:T(512)(128)(2,1)}, u32[]{:S(2)}) copy-start(bf16[512]{0:T(512)(128)(2,1)} %param.12) | copy-start | bytes 3076
  10.9 35.5 %all-to-all-start = ((bf16[8,128,1152]{1,2,0:T(8,128)(2,1)}), bf16[8,128,1152]{1,2,0:T(8,128)(2,1)S(1)}, u32[]{:S(2)}, u32[]{:S(2)}) async-start(bf16[8,128,1152]{1,2,0:T(8,128)(2,1)} %stack.35), calls=%async_computation | async-start | bytes 4718592 | tf_op jit(solution)/shard_map/all_to_all | solution.py:32
  16.4 157.4 %reduce-scatter.3.cloned.1.call-start = ((), (), s32[]{:S(2)}) async-start(), calls=%async_computation.3 | async-start | bytes 11976704 | tf_op jit(solution)/shard_map/reduce_scatter | solution.py:68
  50.6 6.2 %copy-start = (bf16[8,128,1152]{2,1,0:T(8,128)(2,1)S(1)}, bf16[8,128,1152]{2,1,0:T(8,128)(2,1)}, u32[]{:S(2)}) copy-start(bf16[8,128,1152]{2,1,0:T(8,128)(2,1)} %copy.32) | copy-start | bytes 7077892
  50.6 6.2 %copy-start.4 = (bf16[512,3584]{1,0:T(8,128)(2,1)S(1)}, bf16[512,3584]{1,0:T(8,128)(2,1)}, u32[]{:S(2)}) copy-start(bf16[512,3584]{1,0:T(8,128)(2,1)} %param.10) | copy-start | bytes 11010052
  56.8 3.9 %copy-start.5 = (bf16[512,3584]{1,0:T(8,128)(2,1)S(1)}, bf16[512,3584]{1,0:T(8,128)(2,1)}, u32[]{:S(2)}) copy-start(bf16[512,3584]{1,0:T(8,128)(2,1)} %param.9) | copy-start | bytes 11010052
  83.1 188.9 %all-gather.2.cloned.1.call-start = ((), (), s32[]{:S(2)}) async-start(), calls=%async_computation.4 | async-start | bytes 11976704 | tf_op jit(solution)/shard_map/all_gather | solution.py:89
  191.9 122.2 %reduce-scatter.5.cloned.1.call-start = ((), (), s32[]{:S(2)}) async-start(), calls=%async_computation.5 | async-start | bytes 1179648 | tf_op jit(solution)/shard_map/reduce_scatter | solution.py:99
  272.0 4.9 %copy-start.6 = (bf16[512,3584]{1,0:T(8,128)(2,1)S(1)}, bf16[512,3584]{1,0:T(8,128)(2,1)}, u32[]{:S(2)}) copy-start(bf16[512,3584]{1,0:T(8,128)(2,1)} %param.9) | copy-start | bytes 11010052
  276.9 5.3 %copy-start.1 = (bf16[8,128,1152]{2,1,0:T(8,128)(2,1)S(1)}, bf16[8,128,1152]{2,1,0:T(8,128)(2,1)}, u32[]{:S(2)}) copy-start(bf16[8,128,1152]{2,1,0:T(8,128)(2,1)} %copy.32) | copy-start | bytes 7077892
  286.4 12.7 %collective-permute-start.1 = (bf16[256,1792]{1,0:T(8,128)(2,1)S(1)}, bf16[256,1792]{1,0:T(8,128)(2,1)S(1)}, u32[]{:S(2)}, u32[]{:S(2)}) collective-permute-start(bf16[256,1792]{1,0:T(8,128)(2,1)S(1)} %dynamic-slice_convert_fusion), channel_id=1, source_target_pairs={{0,1},{1,0},{2,3},{3,2},{4,5},{5,4},{6,7},{7,6},{8,9},{9,8},{10,11... | collective-permute-start | bytes 2752520 | tf_op jit(solution)/shard_map/ppermute | solution.py:111
  291.0 10.8 %collective-permute-start = (bf16[256,1792]{1,0:T(8,128)(2,1)S(1)}, bf16[256,1792]{1,0:T(8,128)(2,1)S(1)}, u32[]{:S(2)}, u32[]{:S(2)}) collective-permute-start(bf16[256,1792]{1,0:T(8,128)(2,1)S(1)} %dynamic-slice_convert_fusion.1), channel_id=1, source_target_pairs={{0,1},{1,0},{2,3},{3,2},{4,5},{5,4},{6,7},{7,6},{8,9},{9,8},{10,11... | collective-permute-start | bytes 2752520 | tf_op jit(solution)/shard_map/ppermute | solution.py:111
  302.0 12.1 %copy-start.2 = (bf16[128,512]{1,0:T(8,128)(2,1)S(1)}, bf16[128,512]{1,0:T(8,128)(2,1)}, u32[]{:S(2)}) copy-start(bf16[128,512]{1,0:T(8,128)(2,1)} %param.13) | copy-start | bytes 393220
Sparse Core Ops, SparseCore 0:
  83.2 90.6 reduce-scatter.2
  192.0 79.9 all-gather.1
  282.3 31.7 reduce-scatter.4
